TPU v7x, 128 devices: a whole 4x4x4 slice. The times are simulated.
128 devices in a mesh: seq: 32 (over z, y, core), exp: 4 (over x).
Axes of the slice: x: 4, y: 4, z: 4, core: 2. Of those that a mesh axis runs over, the one named last changes fastest.
Arguments:
- residual_in: bfloat16 [16384, 2048], P(('seq', 'exp')), may hold values from -6 to 6
- query_input: bfloat16 [16384, 1024], P(('seq', 'exp')), may hold values from -6 to 6
- key_input: bfloat16 [16384, 1024], P(('seq', 'exp')), may hold values from -6 to 6
- value_input: bfloat16 [16384, 2048], P(('seq', 'exp')), may hold values from -6 to 6
- out_gate: bfloat16 [16384, 2048], P(('seq', 'exp')), may hold values from -6 to 6
- write_strength: float32 [16384, 16], P(('seq', 'exp')), may hold values from 0 to 2
- decay_rate: float32 [16384, 16], P(('seq', 'exp')), may hold values from 0 to 1
- head_gain: float32 [128], replicated, may hold values from 0.1 to 1.9
- out_proj: bfloat16 [2048, 2048], P(None, 'exp'), may hold values from -0.125 to 0.125
- post_gain: float32 [2048], replicated, may hold values from 0.1 to 1.9
- expert_ids: int32 [16384, 10], P(('seq', 'exp')), may hold values from 0 to 255, all different within a row; in each aligned block of 128 rows (0 to 127, 128 to 255, ...) at most 8 rows name the same one
- gate_weights: float32 [16384, 10], P(('seq', 'exp')), may hold values from 0.05 to 0.3
- expert_gate: bfloat16 [256, 2048, 512], P(('seq', 'exp')), may hold values from -0.125 to 0.125
- expert_up: bfloat16 [256, 2048, 512], P(('seq', 'exp')), may hold values from -0.125 to 0.125
- expert_down: bfloat16 [256, 512, 2048], P(('seq', 'exp')), may hold values from -0.25 to 0.25
Outputs:
- layer_out: bfloat16 [16384, 2048], P(('seq', 'exp'))
Inputs may be any that keep to these rules, and one draw needn't show every extreme that they name: `expert_ids`: each row names 10 different experts. Within the rows of one device (aligned blocks of 128 rows) no expert is named more than 8 times, and in every draw some expert is named exactly 8 times within one device's rows.
All inputs are finite; a program needn't handle non-finite values.
Results may differ from a plain program's by a relative error of at most 0.011.
Values may be sent and summed in bfloat16 or wider, within the bound.
A program may use at most 256 MiB of HBM per device.

v0:
```python
from functools import partial

import jax
import jax.numpy as jnp
from jax import lax
from jax.experimental import pallas as pl
from jax.experimental.pallas import tpu as pltpu
from jax.sharding import PartitionSpec as P

D = 2048
HK = 8
HV = 16
DK = 128
DV = 128
TOP = 10
TOGETHER = 1
GROUP = 16

F32 = jnp.float32
BF16 = jnp.bfloat16
MESH = pl.DeviceIdType.MESH


def mm(a, b):
    return jnp.dot(a, b, preferred_element_type=F32)


def mm_t(a, b):
    return lax.dot_general(a, b, (((1,), (1,)), ((), ())), preferred_element_type=F32)


def split(x):
    high = x.astype(BF16)
    return high, (x - high.astype(F32)).astype(BF16)


def mm3(a, b):
    return mm(a[0], b[1]) + mm(jnp.concatenate([a[0], a[1]], axis=1), jnp.concatenate([b[0], b[0]], axis=0))


def mm2(a, b):
    return mm(a[0], b) + mm(a[1], b)


def iota(axis):
    return lax.broadcasted_iota(jnp.int32, (128, 128), axis)


def rows_of(row):
    return jnp.broadcast_to(row, (128, 128))


def unit_inverse(lower):
    row, col = iota(0), iota(1)
    eye = jnp.where(row == col, 1.0, 0.0)
    inverse = eye - jnp.where((row >> 1) == (col >> 1), lower, 0.0)
    for level in range(1, 7):
        mask = ((row >> (level + 1)) == (col >> (level + 1))) & ((row >> level) != (col >> level))
        part = split(jnp.where(mask, lower, 0.0))
        blocks = split(inverse)
        inverse = inverse - mm3(blocks, split(mm3(part, blocks)))
    return inverse


def mixer_kernel(
    seq_size,
    exp_size,
    stride,
    q_hbm,
    k_hbm,
    v_hbm,
    gate_hbm,
    residual_hbm,
    proj_hbm,
    rate_ref,
    beta_ref,
    gain_ref,
    post_gain_ref,
    hidden_ref,
    normed_ref,
    q_ref,
    k_ref,
    v_ref,
    gate_ref,
    residual_ref,
    proj,
    core_out,
    logs,
    local_out,
    query_high,
    query_low,
    maps,
    adds,
    maps_in,
    adds_in,
    prefix,
    prefix_add,
    last_map,
    last_add,
    groups_in,
    groups_add,
    states,
    states_in,
    load,
    send1,
    recv1,
    send2,
    recv2,
    send3,
    recv3,
    proj_send,
    proj_recv,
):
    lines = GROUP // exp_size
    groups = seq_size // lines
    seq, exp = lax.axis_index("seq"), lax.axis_index("exp")
    group = seq // lines
    rank = (seq % lines) * exp_size + exp

    loads = [
        pltpu.make_async_copy(source, target, load.at[number])
        for number, (source, target) in enumerate(
            [
                (k_hbm, k_ref),
                (q_hbm, q_ref),
                (v_hbm, v_ref),
                (gate_hbm, gate_ref),
                (residual_hbm, residual_ref),
                (proj_hbm, proj.at[exp]),
            ]
        )
    ]
    for copy in loads:
        copy.start()

    def device(of_group, of_rank):
        return (of_group * lines + of_rank // exp_size, of_rank % exp_size)

    core = seq % 2
    spot = (seq // stride) % 4

    def ring_seq(shift):
        return seq + ((spot + shift) % 4 - spot) * stride

    def ring_exp(shift):
        return lax.rem(exp + shift, 4)

    partner = (seq + 1 - 2 * core, exp)
    rows = proj_hbm.shape[0] // 8
    half = rows // 2

    def piece(x_shift, spot_shift, begin, size):
        row = pl.multiple_of(core * (4 * rows) + (spot + spot_shift) % 4 * rows + begin, half)
        return proj.at[ring_exp(x_shift), pl.ds(row, size)]

    counter = [0]

    def proj_copy(ref, recv_index, to, source=None):
        number = counter[0]
        counter[0] += 1
        return pltpu.make_async_remote_copy(
            src_ref=ref if source is None else source,
            dst_ref=ref,
            send_sem=proj_send.at[number],
            recv_sem=proj_recv.at[recv_index],
            device_id=to,
            device_id_type=MESH,
        )

    def landing(ref, recv_index):
        return pltpu.make_async_copy(ref, ref, proj_recv.at[recv_index])

    own = proj_hbm.at[pl.ds(pl.multiple_of(core * (4 * rows) + spot * rows, half), rows)]
    mine = piece(0, 0, 0, rows)
    right, left = (seq, ring_exp(1)), (seq, ring_exp(3))
    above, below = (ring_seq(1), exp), (ring_seq(3), exp)
    x_first = [proj_copy(mine, 0, right, own), proj_copy(mine, 1, left, own)]
    x_second = [proj_copy(piece(3, 0, 0, half), 2, right), proj_copy(piece(1, 0, half, half), 3, left)]
    x_landing = [
        landing(piece(3, 0, 0, rows), 0),
        landing(piece(1, 0, 0, rows), 1),
        landing(piece(2, 0, 0, half), 2),
        landing(piece(2, 0, half, half), 3),
    ]
    shifts = (3, 1, 2)
    z_first, z_second, z_landing, across, across_landing = [], [], [], [], []
    for number, shift in enumerate(shifts):
        at = 4 + 4 * number
        z_first.append(
            [proj_copy(piece(shift, 0, 0, rows), at, above), proj_copy(piece(shift, 0, 0, rows), at + 1, below)]
        )
        z_second.append(
            [proj_copy(piece(shift, 3, 0, half), at + 2, above), proj_copy(piece(shift, 1, half, half), at + 3, below)]
        )
        z_landing.append(
            [
                landing(piece(shift, 3, 0, rows), at),
                landing(piece(shift, 1, 0, rows), at + 1),
                landing(piece(shift, 2, 0, half), at + 2),
                landing(piece(shift, 2, half, half), at + 3),
            ]
        )
        across.append([proj_copy(piece(shift, n, 0, rows), 16 + 4 * number + n, partner) for n in range(4)])
        other = (1 - core) * (4 * rows)
        across_landing.append(
            [
                landing(
                    proj.at[
                        ring_exp(shift), pl.ds(pl.multiple_of(other + (spot + n) % 4 * rows, half), rows)
                    ],
                    16 + 4 * number + n,
                )
                for n in range(4)
            ]
        )

    barrier = pltpu.get_barrier_semaphore()

    def greet(to):
        pl.semaphore_signal(barrier, inc=1, device_id=to, device_id_type=MESH)

    def greet_rank(step, carry):
        greet(device(group, lax.rem(rank + step, GROUP)))
        return carry

    def greet_group(step, carry):
        greet(device(lax.rem(group + step, groups), rank))
        return carry

    lax.fori_loop(1, GROUP, greet_rank, 0)
    lax.fori_loop(1, groups, greet_group, 0)
    for to in (right, left, above, below, partner):
        greet(to)
    pl.semaphore_wait(barrier, GROUP - 1 + groups - 1 + 5)

    for copy in x_first:
        copy.start()

    row, col = iota(0), iota(1)
    upto = jnp.where(row <= col, 1.0, 0.0).astype(BF16)
    rate = rate_ref[...]
    first, rest = split(rate)
    last = (rate - first.astype(F32) - rest.astype(F32)).astype(BF16)
    logs[...] = -(mm(first, upto) + (mm(rest, upto) + mm(last, upto)))
    for copy in loads[:3]:
        copy.wait()

    def map_copies(head, to):
        return [
            pltpu.make_async_remote_copy(
                src_ref=source.at[head],
                dst_ref=target.at[to],
                send_sem=send1.at[number, head],
                recv_sem=recv1.at[number, to],
                device_id=device(group, head),
                device_id_type=MESH,
            )
            for number, (source, target) in enumerate([(maps, maps_in), (adds, adds_in)])
        ]

    def map_keeps(head, to):
        return [
            pltpu.make_async_copy(maps.at[head], maps_in.at[to], recv1.at[0, to]),
            pltpu.make_async_copy(adds.at[head], adds_in.at[to], recv1.at[1, to]),
        ]

    def key_head(kh):
        columns = pl.ds(pl.multiple_of(kh * DK, DK), DK)
        k_raw, q_raw = k_ref[:, columns], q_ref[:, columns]
        k_wide, q_wide = k_raw.astype(F32), q_raw.astype(F32)
        k_inv = lax.rsqrt(jnp.sum(k_wide * k_wide, axis=1, keepdims=True) + 1e-6)
        q_inv = lax.rsqrt(jnp.sum(q_wide * q_wide, axis=1, keepdims=True) + 1e-6) * DK ** (-0.5)
        k_inv = jnp.broadcast_to(k_inv, (128, 128))
        k_inv_row = k_inv.T
        k_t = k_wide.T.astype(BF16)
        gram = mm_t(k_raw, k_raw) * k_inv * k_inv_row
        mixed = mm_t(q_raw, k_raw) * q_inv * k_inv_row
        for part in range(HV // HK):
            h = kh * (HV // HK) + part
            head_columns = pl.ds(pl.multiple_of(h * DV, DV), DV)
            log_row = rows_of(logs[pl.ds(h, 1), :])
            log_col = log_row.T
            beta_row = rows_of(beta_ref[pl.ds(h, 1), :])
            beta_col = beta_row.T
            ratio = jnp.where(row >= col, jnp.exp(jnp.where(row >= col, log_col - log_row, 0.0)), 0.0)
            inverse = unit_inverse(jnp.where(row > col, ratio * gram, 0.0) * beta_col)
            v_raw = v_ref[:, head_columns]
            weights = split(inverse * beta_row)
            newest = mm2(weights, v_raw)
            weights = split(inverse * (beta_row * jnp.exp(log_row) * k_inv_row))
            key_matrix = mm2(weights, k_raw)
            log_last = jnp.broadcast_to(logs[pl.ds(h, 1), 127:128], (128, 128))
            fade = k_inv * jnp.exp(log_last - log_col)
            side = split(key_matrix * fade)
            moved = mm(k_t, side[0]) + mm(k_t, side[1])
            maps[h] = jnp.where(row == col, jnp.exp(log_last), 0.0) - moved
            side = split(newest * fade)
            adds[h] = (mm(k_t, side[0]) + mm(k_t, side[1])).astype(BF16)
            mix = split(mixed * ratio)
            local_out[h] = mm3(mix, split(newest))
            effective = split(q_wide * q_inv * jnp.exp(log_col) - mm3(mix, split(key_matrix)))
            query_high[h] = effective[0]
            query_low[h] = effective[1]

    def key_heads(step, carry):
        for part in range(TOGETHER):
            key_head(step * TOGETHER + part)
        for part in range(TOGETHER * (HV // HK)):
            h = step * (TOGETHER * (HV // HK)) + part

            @pl.when(h != rank)
            def _():
                for copy in map_copies(h, rank):
                    copy.start()

            @pl.when(h == rank)
            def _():
                for copy in map_keeps(h, rank):
                    copy.start()

        @pl.when(step == 1)
        def _():
            for copy in x_landing[:2]:
                copy.wait()
            for copy in x_second + z_first[0] + z_first[1] + [across[0][0], across[1][0]]:
                copy.start()

        @pl.when(step == HK // TOGETHER - 2)
        def _():
            for copy in x_landing[2:]:
                copy.wait()
            for copy in z_first[2] + [across[2][0]]:
                copy.start()

        return carry

    lax.fori_loop(0, HK // TOGETHER, key_heads, 0)

    for number in range(3):
        for copy in z_landing[number][:2]:
            copy.wait()
        for copy in z_second[number] + [across[number][3], across[number][1]]:
            copy.start()

    middle = GROUP // 2
    for start in (0, middle):
        for copy in map_keeps(start, start):
            copy.wait()
        prefix[start] = maps_in[start]
        prefix_add[start] = adds_in[start].astype(F32)

    def chain(step, carry):
        for start in (0, middle):
            index = start + step
            for copy in map_keeps(index, index):
                copy.wait()
        for start in (0, middle):
            index = start + step
            moved = split(maps_in[index])
            prefix[index] = mm3(moved, split(prefix[index - 1]))
            prefix_add[index] = mm3(moved, split(prefix_add[index - 1])) + adds_in[index].astype(F32)
        return carry

    lax.fori_loop(1, middle, chain, 0)
    moved = split(prefix[GROUP - 1])
    last_map[...] = mm3(moved, split(prefix[middle - 1]))
    last_add[...] = (mm3(moved, split(prefix_add[middle - 1])) + prefix_add[GROUP - 1]).astype(BF16)

    def group_copies(to, source):
        return [
            pltpu.make_async_remote_copy(
                src_ref=kept,
                dst_ref=target.at[source],
                send_sem=send2.at[number, to],
                recv_sem=recv2.at[number, source],
                device_id=device(to, rank),
                device_id_type=MESH,
            )
            for number, (kept, target) in enumerate([(last_map, groups_in), (last_add, groups_add)])
        ]

    def send_group(to, carry):
        for copy in group_copies(to, group):
            copy.start()
        return carry

    lax.fori_loop(group + 1, groups, send_group, 0)

    for number in range(3):
        for copy in z_landing[number][2:]:
            copy.wait()
        across[number][2].start()

    def enter(source, state):
        for copy in group_copies(group, source):
            copy.wait_recv()
        return mm3(split(groups_in[source]), split(state)) + groups_add[source].astype(F32)

    entering = split(lax.fori_loop(0, group, enter, jnp.zeros((DK, DV), F32)))
    halfway = split(mm3(split(prefix[middle - 1]), entering) + prefix_add[middle - 1])

    def state_copy(to, head):
        return pltpu.make_async_remote_copy(
            src_ref=states.at[to],
            dst_ref=states_in.at[head],
            send_sem=send3.at[to],
            recv_sem=recv3.at[head],
            device_id=device(group, to),
            device_id_type=MESH,
        )

    def state_keep(to, head):
        return pltpu.make_async_copy(states.at[to], states_in.at[head], recv3.at[head])

    def give(to):
        @pl.when(to != rank)
        def _():
            state_copy(to, rank).start()

        @pl.when(to == rank)
        def _():
            state_keep(to, rank).start()

    states[0] = entering[0]
    states[middle] = halfway[0]
    give(0)
    give(middle)

    def spread(step, carry):
        for start, state in ((0, entering), (middle, halfway)):
            index = start + step
            moved = mm3(split(prefix[index - 1]), state) + prefix_add[index - 1]
            states[index] = moved.astype(BF16)
        for start in (0, middle):
            give(start + step)
        return carry

    lax.fori_loop(1, middle, spread, 0)

    gain = gain_ref[...]
    loads[3].wait()

    def finish(h, carry):
        columns = pl.ds(pl.multiple_of(h * DV, DV), DV)
        gate = gate_ref[:, columns].astype(F32)
        scale = gain * (gate / (1.0 + jnp.exp(-gate)))
        state_keep(h, h).wait()
        state = states_in[h]
        out = local_out[h] + (mm(query_high[h], state) + mm(query_low[h], state))
        inv_rms = lax.rsqrt(jnp.sum(out * out, axis=1, keepdims=True) * (1.0 / DV) + 1e-6)
        core_out[:, columns] = (out * inv_rms * scale).astype(BF16)
        return carry

    lax.fori_loop(0, HV, finish, 0, unroll=4)

    loads[4].wait()
    loads[5].wait()
    for number in range(3):
        for copy in across_landing[number]:
            copy.wait()
    width = proj_hbm.shape[1]

    def project(index, square):
        columns = pl.ds(pl.multiple_of(index * width, width), width)
        mixed = mm(core_out[...], proj[index])
        hidden = (residual_ref[:, columns].astype(F32) + mixed).astype(BF16)
        hidden_ref[:, columns] = hidden
        wide = hidden.astype(F32)
        return square + jnp.sum(wide * wide, axis=1, keepdims=True)

    square = lax.fori_loop(0, exp_size, project, jnp.zeros((128, 1), F32))
    inv_rms = lax.rsqrt(square * (1.0 / D) + 1e-6)
    normed_ref[...] = (hidden_ref[...].astype(F32) * inv_rms * post_gain_ref[...]).astype(BF16)

    def drain(index, carry):
        @pl.when(index != rank)
        def _():
            for copy in map_copies(index, rank):
                copy.wait_send()
            state_copy(index, rank).wait_send()

        return carry

    lax.fori_loop(0, GROUP, drain, 0)

    def drain_group(to, carry):
        for copy in group_copies(to, group):
            copy.wait_send()
        return carry

    lax.fori_loop(group + 1, groups, drain_group, 0)
    for copy in x_first + x_second:
        copy.wait_send()
    for number in range(3):
        for copy in z_first[number] + z_second[number] + across[number]:
            copy.wait_send()


def mixer(query, key, value, gate, residual, proj, strength, rate, head_gain, post_gain, stride):
    seq_size, exp_size = lax.axis_size("seq"), lax.axis_size("exp")
    groups = seq_size * exp_size // GROUP
    tokens = query.shape[0]
    vmem = pl.BlockSpec(memory_space=pltpu.VMEM)
    hbm = pl.BlockSpec(memory_space=pl.ANY)
    square = (128, 128)
    return pl.pallas_call(
        partial(mixer_kernel, seq_size, exp_size, stride),
        out_shape=[jax.ShapeDtypeStruct((tokens, D), BF16)] * 2,
        in_specs=[hbm] * 6 + [vmem] * 4,
        out_specs=[vmem, vmem],
        scratch_shapes=[
            pltpu.VMEM(query.shape, BF16),
            pltpu.VMEM(key.shape, BF16),
            pltpu.VMEM(value.shape, BF16),
            pltpu.VMEM(gate.shape, BF16),
            pltpu.VMEM(residual.shape, BF16),
            pltpu.VMEM((exp_size,) + proj.shape, BF16),
            pltpu.VMEM(value.shape, BF16),
            pltpu.VMEM((HV, tokens), F32),
            pltpu.VMEM((HV,) + square, F32),
            pltpu.VMEM((HV,) + square, BF16),
            pltpu.VMEM((HV,) + square, BF16),
            pltpu.VMEM((HV,) + square, F32),
            pltpu.VMEM((HV,) + square, BF16),
            pltpu.VMEM((GROUP,) + square, F32),
            pltpu.VMEM((GROUP,) + square, BF16),
            pltpu.VMEM((GROUP,) + square, F32),
            pltpu.VMEM((GROUP,) + square, F32),
            pltpu.VMEM(square, F32),
            pltpu.VMEM(square, BF16),
            pltpu.VMEM((groups,) + square, F32),
            pltpu.VMEM((groups,) + square, BF16),
            pltpu.VMEM((GROUP,) + square, BF16),
            pltpu.VMEM((HV,) + square, BF16),
            pltpu.SemaphoreType.DMA((6,)),
            pltpu.SemaphoreType.DMA((2, HV)),
            pltpu.SemaphoreType.DMA((2, GROUP)),
            pltpu.SemaphoreType.DMA((2, groups)),
            pltpu.SemaphoreType.DMA((2, groups)),
            pltpu.SemaphoreType.DMA((GROUP,)),
            pltpu.SemaphoreType.DMA((HV,)),
            pltpu.SemaphoreType.DMA((28,)),
            pltpu.SemaphoreType.DMA((28,)),
        ],
        compiler_params=pltpu.CompilerParams(
            collective_id=0, has_side_effects=True, vmem_limit_bytes=56 * 1024 * 1024
        ),
        cost_estimate=pl.CostEstimate(flops=8_000_000_000, bytes_accessed=4_000_000, transcendentals=0),
    )(
        query,
        key,
        value,
        gate,
        residual,
        proj,
        rate.T,
        strength.T,
        head_gain.reshape(1, DV),
        post_gain.reshape(1, D),
    )


PARTS = ((0, 1, 2), (1, 2, 0), (2, 0, 1))
BEGIN = (0, 640, 1280)
WIDTH = (640, 640, 768)
EXTRA = 8
BLOCK = 128 + EXTRA


class Torus:
    def __init__(self):
        seq, self.exp = lax.axis_index("seq"), lax.axis_index("exp")
        self.core = seq % 2
        self.at = (self.exp, (seq // 2) % 4, seq // 8)

    def place(self, axis, shift, core=None):
        x, y, z = [(c + shift) % 4 if n == axis else c for n, c in enumerate(self.at)]
        return ((z * 4 + y) * 2 + (self.core if core is None else core), x)

    def partner(self):
        return self.place(0, 0, 1 - self.core)

    def greet(self):
        barrier = pltpu.get_barrier_semaphore()
        others = [self.partner()]
        for axis in range(3):
            for shift in (1, 3):
                others += [self.place(axis, shift), self.place(axis, shift, 1 - self.core)]
        for to in others:
            pl.semaphore_signal(barrier, inc=1, device_id=to, device_id_type=MESH)
        pl.semaphore_wait(barrier, len(others))


class Sends:
    def __init__(self, send, recv):
        self.send, self.recv, self.count, self.open = send, recv, 0, []

    def go(self, source, target, index, to):
        copy = pltpu.make_async_remote_copy(
            src_ref=source,
            dst_ref=target,
            send_sem=self.send.at[self.count],
            recv_sem=self.recv.at[index],
            device_id=to,
            device_id_type=MESH,
        )
        self.count += 1
        copy.start()
        self.open.append(copy)

    def keep(self, source, target, index):
        pltpu.make_async_copy(source, target, self.recv.at[index]).start()

    def landed(self, target, index):
        pltpu.make_async_copy(target, target, self.recv.at[index]).wait()

    def finish(self):
        for copy in self.open:
            copy.wait_send()


def view(ref, expert, core, columns, chosen):
    x, y, z = [chosen.get(axis, slice(None)) for axis in range(3)]
    return ref.at[z, expert, x, y, core, slice(None), columns]


def ordered(part, second, first):
    return (second, first) if part == 0 else (first, second)


def slots(expert):
    return pl.ds(8 * expert, 8)


def dispatch_kernel(normed_ref, ids_ref, weight_ref, out_ref, mix_ref, extra, *scratch):
    blocks, rows_out = scratch[0:3], scratch[3:6]
    from_left, from_right = scratch[6:9], scratch[9:12]
    sends = Sends(scratch[12], scratch[13])
    torus = Torus()
    extra[...] = jnp.full(extra.shape, -1.0, F32)
    extra[0, :TOP] = ids_ref[...].astype(F32)
    extra[1, :TOP] = weight_ref[...]
    for p in range(3):
        columns = pl.ds(BEGIN[p], WIDTH[p])
        blocks[p][0, 0, :128, :] = normed_ref[:, columns]
        for number in range(4):
            lanes = slice(128 * number, 128 * (number + 1))
            rows = slice(8 * (number % 2), 8 * (number % 2) + 8)
            blocks[p][0, 0, 128:, lanes] = extra[number // 2, rows].astype(BF16)
        blocks[p][0, 0, 128:, 512:] = jnp.zeros((EXTRA, WIDTH[p] - 512), BF16)
    torus.greet()
    low, high = pl.ds(0, 72), pl.ds(72, BLOCK - 72)

    def hand_on(p, first):
        b = PARTS[p][2]
        block = blocks[p].at[0, first]
        sends.go(block, blocks[p].at[3, first], 64 * p + 4 + first, torus.place(b, 1))
        sends.go(block, blocks[p].at[1, first], 64 * p + 8 + first, torus.place(b, 3))

    def gathered(p, second, first):
        sends.landed(blocks[p].at[second, first], 64 * p + (4 if second == 3 else 8) + first)

    for p, (_, a, b) in enumerate(PARTS):
        own = blocks[p].at[0, 0]
        sends.go(own, blocks[p].at[0, 3], 64 * p + 0, torus.place(a, 1))
        sends.go(own, blocks[p].at[0, 1], 64 * p + 1, torus.place(a, 3))
    for p in range(3):
        hand_on(p, 0)
    for p, (_, a, b) in enumerate(PARTS):
        sends.landed(blocks[p].at[0, 3], 64 * p + 0)
        sends.go(blocks[p].at[0, 3, low], blocks[p].at[0, 2, low], 64 * p + 2, torus.place(a, 1))
        sends.landed(blocks[p].at[0, 1], 64 * p + 1)
        sends.go(blocks[p].at[0, 1, high], blocks[p].at[0, 2, high], 64 * p + 3, torus.place(a, 3))
        hand_on(p, 1)
        hand_on(p, 3)
    for p in range(3):
        sends.landed(blocks[p].at[0, 2, low], 64 * p + 2)
        sends.landed(blocks[p].at[0, 2, high], 64 * p + 3)
        hand_on(p, 2)

    row, col = iota(0), iota(1)
    earlier = jnp.where(row < col, 1.0, 0.0).astype(BF16)
    spread_row = lax.broadcasted_iota(jnp.int32, (128, 16), 0)
    spread_col = lax.broadcasted_iota(jnp.int32, (128, 16), 1)
    spread = jnp.where((spread_row >> 3) == spread_col, 1.0, 0.0).astype(BF16)
    slot = (row & 7).astype(F32)
    line = lax.broadcasted_iota(jnp.int32, (16, 128), 0)

    def extract(p, second):
        place = [(c + (line >> 2)) & 3 if n == PARTS[p][0] else c for n, c in enumerate(torus.at)]
        device = ((place[2] * 4 + place[1]) * 2 + ((line >> 1) & 1)) * 4 + place[0]
        expert = (device * 2 + (line & 1)).astype(F32)

        def one(first, carry):
            block = blocks[p].at[second, first]
            extras = [block[128:, 128 * n : 128 * (n + 1)].astype(F32) for n in range(4)]
            named = jnp.zeros((16, 128), F32)
            weight = jnp.zeros((16, 128), F32)
            for choice in range(TOP):
                number, at = choice // 8, slice(choice % 8, choice % 8 + 1)
                hit = expert == jnp.broadcast_to(extras[number][at, :], (16, 128))
                named = jnp.where(hit, 1.0, named)
                weight = jnp.where(hit, jnp.broadcast_to(extras[2 + number][at, :], (16, 128)), weight)
            before = mm(named.astype(BF16), earlier)
            code = jnp.where(named > 0.5, before, -1.0).astype(BF16)
            here = mm(spread, code) == slot
            pick = jnp.where(here, 1.0, 0.0).astype(BF16)
            mix = jnp.where(here, mm(spread, weight.astype(BF16)), 0.0)
            mix_ref[p, second * 4 + first] = mix.T.astype(BF16)
            taken = mm(pick, block[:128, :]).astype(BF16).reshape(8, 16, WIDTH[p])
            i, k = ordered(p, second, first)
            rows_out[p][:, i, k] = taken
            return carry

        lax.fori_loop(0, 4, one, 0, unroll=True)

    core = torus.core

    def chunk(p, second):
        return (second,) if p == 0 else (slice(None), second)

    def slot_of(p, place, of_core, second):
        return 64 * p + 24 + place * 8 + of_core * 4 + second

    def columns_of(p):
        return pl.ds(BEGIN[p], WIDTH[p])

    def every(p):
        return (slice(None),) if p == 0 else ()

    def send_chunk(p, second):
        axis, _, b = PARTS[p]
        rows = rows_out[p]
        for number, (relay, shift) in enumerate(((from_left[p], 1), (from_right[p], 3))):
            sends.go(
                rows.at[(4 + number,) + chunk(p, second)],
                relay.at[chunk(p, second)],
                64 * p + 14 + number * 4 + second,
                torus.place(axis, shift),
            )
        for e in range(2):

            def source(line):
                return rows.at[(line,) + chunk(p, second) + every(p) + (slots(e),)]

            for shift in (1, 3):
                for to_core in range(2):
                    sends.go(
                        source(2 * shift + to_core),
                        view(out_ref, e, core, columns_of(p), {axis: 4 - shift, b: second}),
                        slot_of(p, 4 - shift, core, second),
                        torus.place(axis, shift, to_core),
                    )
            here = view(out_ref, e, core, columns_of(p), {axis: 0, b: second})
            sends.go(source(1 - core), here, slot_of(p, 0, core, second), torus.partner())
            sends.keep(source(core), here, slot_of(p, 0, core, second))

    def pass_on(p, second):
        axis, _, b = PARTS[p]
        for number, (relay, shift) in enumerate(((from_left[p], 1), (from_right[p], 3))):
            sends.landed(relay.at[chunk(p, second)], 64 * p + 14 + number * 4 + second)
            for e in range(2):
                sends.go(
                    relay.at[chunk(p, second) + every(p) + (slots(e),)],
                    view(out_ref, e, core, columns_of(p), {axis: 2, b: second}),
                    slot_of(p, 2, core, second),
                    torus.place(axis, shift, number),
                )

    for p in range(3):
        extract(p, 0)
        send_chunk(p, 0)
    for p, (_, a, b) in enumerate(PARTS):
        gathered(p, 3, 0)
        gathered(p, 3, 1)
        sends.go(blocks[p].at[3, 0:2], blocks[p].at[2, 0:2], 64 * p + 12, torus.place(b, 1))
        gathered(p, 1, 3)
        gathered(p, 1, 2)
        sends.go(blocks[p].at[1, 2:4], blocks[p].at[2, 2:4], 64 * p + 13, torus.place(b, 3))
    for p in range(3):
        gathered(p, 3, 3)
        gathered(p, 3, 2)
        extract(p, 3)
        send_chunk(p, 3)
    for p in range(3):
        gathered(p, 1, 0)
        gathered(p, 1, 1)
        extract(p, 1)
        send_chunk(p, 1)
        pass_on(p, 0)
    for p in range(3):
        sends.landed(blocks[p].at[2, 0:2], 64 * p + 12)
        sends.landed(blocks[p].at[2, 2:4], 64 * p + 13)
        extract(p, 2)
        send_chunk(p, 2)
        pass_on(p, 3)
    for second in (1, 2):
        for p in range(3):
            pass_on(p, second)
    both = slice(None)
    for p, (axis, a, b) in enumerate(PARTS):
        for place in range(4):
            for of_core in range(2):
                for second in range(4):
                    sends.landed(
                        view(out_ref, both, of_core, columns_of(p), {axis: place, b: second}),
                        slot_of(p, place, of_core, second),
                    )
    sends.finish()


def dispatch(normed, ids, weights):
    vmem = pl.BlockSpec(memory_space=pltpu.VMEM)
    hbm = pl.BlockSpec(memory_space=pl.ANY)
    return pl.pallas_call(
        dispatch_kernel,
        out_shape=[
            jax.ShapeDtypeStruct((4, 2, 4, 4, 2, 8, D), BF16),
            jax.ShapeDtypeStruct((3, 16, 128, 128), BF16),
        ],
        in_specs=[vmem] * 3,
        out_specs=[hbm, vmem],
        scratch_shapes=[pltpu.VMEM((2, 16, 128), F32)]
        + [pltpu.VMEM((4, 4, BLOCK, w), BF16) for w in WIDTH]
        + [pltpu.VMEM((8, 4, 4, 16, w), BF16) for w in WIDTH]
        + [pltpu.VMEM((4, 4, 16, w), BF16) for w in WIDTH] * 2
        + [pltpu.SemaphoreType.DMA((240,)), pltpu.SemaphoreType.DMA((192,))],
        compiler_params=pltpu.CompilerParams(
            collective_id=1, has_side_effects=True, vmem_limit_bytes=58 * 1024 * 1024
        ),
        cost_estimate=pl.CostEstimate(flops=2_000_000_000, bytes_accessed=10_000_000, transcendentals=0),
    )(normed, ids, weights)


CHUNKS = (2, 1, 3, 0)


def combine_kernel(
    rows_hbm,
    gate_hbm,
    up_hbm,
    down_hbm,
    mix_ref,
    hidden_ref,
    out_ref,
    rows_ref,
    inner_ref,
    gate_ref,
    up_ref,
    down_ref,
    load,
    fetch,
    *scratch,
):
    rows_in, from_left, from_right = scratch[0:3], scratch[3:6], scratch[6:9]
    sums, over, under, add_over, add_under = (
        scratch[9:12],
        scratch[12:15],
        scratch[15:18],
        scratch[18:21],
        scratch[21:24],
    )
    sends = Sends(scratch[24], scratch[25])
    torus = Torus()
    core = torus.core
    loads = [pltpu.make_async_copy(rows_hbm.at[k], rows_ref.at[k], load.at[k]) for k in range(4)]
    weights = [
        [
            pltpu.make_async_copy(source.at[e], target.at[e], fetch.at[number, e])
            for number, (source, target) in enumerate(((gate_hbm, gate_ref), (up_hbm, up_ref), (down_hbm, down_ref)))
        ]
        for e in range(2)
    ]
    loads[CHUNKS[0]].start()
    for copy in weights[0] + weights[1]:
        copy.start()
    for k in CHUNKS[1:]:
        loads[k].start()
    torus.greet()

    def expert(k, e):
        if k == CHUNKS[0]:
            for copy in weights[e]:
                copy.wait()
        block = rows_ref.at[k, e].reshape(256, D)

        def widen(step, carry):
            columns = pl.ds(pl.multiple_of(step * 256, 256), 256)
            gate_part = mm(block[...], gate_ref[e, :, columns])
            up_part = mm(block[...], up_ref[e, :, columns])
            inner_ref[:, columns] = (gate_part / (1.0 + jnp.exp(-gate_part)) * up_part).astype(BF16)
            return carry

        lax.fori_loop(0, 2, widen, 0)

        def narrow(step, carry):
            columns = pl.ds(pl.multiple_of(step * 512, 512), 512)
            block[:, columns] = mm(inner_ref[...], down_ref[e, :, columns]).astype(BF16)
            return carry

        lax.fori_loop(0, 4, narrow, 0)

    def region(p, k):
        return () if p == 2 else (k,)

    def slot_of(p, line, k):
        return 64 * p + line * 4 + (0 if p == 2 else k)

    def relay_slot(p, number, k):
        return 64 * p + 32 + number * 4 + (0 if p == 2 else k)

    def send_chunk(k, e):
        for p, (axis, a, b) in enumerate(PARTS):
            columns = pl.ds(BEGIN[p], WIDTH[p])
            every = (slice(None),) * (2 if p == 2 else 1)
            for shift in (k,) if p == 2 else CHUNKS:
                chosen = {2: k} if p == 2 else {axis: shift, 2: k}

                def source(of_core):
                    return view(rows_ref, e, of_core, columns, chosen)

                def target(ref):
                    return ref.at[region(p, k) + every + (slots(e),)]

                line = rows_in[p].at[2 * ((4 - shift) % 4) + core]
                index = slot_of(p, 2 * ((4 - shift) % 4) + core, k)
                if shift == 2:
                    sends.go(source(0), target(from_left[p]), relay_slot(p, 0, k), torus.place(axis, 1))
                    sends.go(source(1), target(from_right[p]), relay_slot(p, 1, k), torus.place(axis, 3))
                elif shift == 0:
                    sends.go(source(1 - core), target(line), index, torus.partner())
                    sends.keep(source(core), target(line), index)
                else:
                    for of_core in range(2):
                        sends.go(source(of_core), target(line), index, torus.place(axis, shift, of_core))

    def pass_on(p, k):
        axis = PARTS[p][0]
        for number, (relay, shift) in enumerate(((from_left[p], 1), (from_right[p], 3))):
            part = relay.at[region(p, k)] if p != 2 else relay
            sends.landed(part, relay_slot(p, number, k))
            sends.go(
                part,
                rows_in[p].at[(4 + core,) + region(p, k)],
                slot_of(p, 4 + core, k),
                torus.place(axis, shift, number),
            )

    def arrived(p, k):
        for line in range(8):
            sends.landed(rows_in[p].at[(line,) + region(p, k)], slot_of(p, line, k))

    before = None
    for k in CHUNKS:
        loads[k].wait()
        expert(k, 0)
        send_chunk(k, 0)
        expert(k, 1)
        if before is not None:
            for p in range(2):
                pass_on(p, before)
            if before == 2:
                pass_on(2, 2)
        send_chunk(k, 1)
        before = k
    for p in range(2):
        pass_on(p, before)

    def add_up(p, second):
        def one(first, carry):
            i, k = ordered(p, second, first)
            rows = rows_in[p][:, i, k].reshape(128, WIDTH[p])
            sums[p][second, first] = mm(mix_ref[p, second * 4 + first], rows).astype(BF16)
            return carry

        lax.fori_loop(0, 4, one, 0, unroll=True)

    def first_sums(p):
        b = PARTS[p][2]
        add_up(p, 2)
        sends.go(sums[p].at[2, 0:2], add_over[p], 64 * p + 42, torus.place(b, 1))
        sends.go(sums[p].at[2, 2:4], add_under[p], 64 * p + 43, torus.place(b, 3))

    arrived(0, 2)
    first_sums(0)
    for p in range(3):
        if p == 2:
            arrived(2, 0)
        else:
            for k in CHUNKS[1:] if p == 0 else CHUNKS:
                arrived(p, k)
        if p > 0:
            first_sums(p)
    for p, (axis, a, b) in enumerate(PARTS):
        add_up(p, 1)
        sends.go(sums[p].at[1, 2:4], over[p].at[2:4], 64 * p + 44, torus.place(b, 1))
        add_up(p, 3)
        sends.go(sums[p].at[3, 0:2], under[p].at[0:2], 64 * p + 45, torus.place(b, 3))
    for p, (axis, a, b) in enumerate(PARTS):
        sends.landed(add_over[p], 64 * p + 42)
        sums[p][1, 0:2] = (sums[p][1, 0:2].astype(F32) + add_over[p][...].astype(F32)).astype(BF16)
        sends.go(sums[p].at[1, 0:2], over[p].at[0:2], 64 * p + 46, torus.place(b, 1))
        sends.landed(add_under[p], 64 * p + 43)
        sums[p][3, 2:4] = (sums[p][3, 2:4].astype(F32) + add_under[p][...].astype(F32)).astype(BF16)
        sends.go(sums[p].at[3, 2:4], under[p].at[2:4], 64 * p + 47, torus.place(b, 3))
    for p in range(3):
        add_up(p, 0)
    low, high = pl.ds(0, 64), pl.ds(64, 64)
    for p, (axis, a, b) in enumerate(PARTS):
        sends.landed(over[p].at[2:4], 64 * p + 44)
        sends.landed(under[p].at[0:2], 64 * p + 45)
        sends.landed(over[p].at[0:2], 64 * p + 46)
        sends.landed(under[p].at[2:4], 64 * p + 47)
        for first in (2, 1, 3, 0):
            total = sums[p][0, first].astype(F32) + over[p][first].astype(F32) + under[p][first].astype(F32)
            sums[p][0, first] = total.astype(BF16)
            if first == 2:
                sends.go(sums[p].at[0, 2, low], over[p].at[4, low], 64 * p + 48, torus.place(a, 1))
                sends.go(sums[p].at[0, 2, high], under[p].at[4, high], 64 * p + 49, torus.place(a, 3))
            elif first == 1:
                sends.go(sums[p].at[0, 1, high], over[p].at[5, high], 64 * p + 50, torus.place(a, 1))
            elif first == 3:
                sends.go(sums[p].at[0, 3, low], under[p].at[5, low], 64 * p + 51, torus.place(a, 3))
    for p, (axis, a, b) in enumerate(PARTS):
        sends.landed(over[p].at[4, low], 64 * p + 48)
        sums[p][0, 1, :64] = (sums[p][0, 1, :64].astype(F32) + over[p][4, :64].astype(F32)).astype(BF16)
        sends.go(sums[p].at[0, 1, low], over[p].at[5, low], 64 * p + 52, torus.place(a, 1))
        sends.landed(under[p].at[4, high], 64 * p + 49)
        sums[p][0, 3, 64:] = (sums[p][0, 3, 64:].astype(F32) + under[p][4, 64:].astype(F32)).astype(BF16)
        sends.go(sums[p].at[0, 3, high], under[p].at[5, high], 64 * p + 53, torus.place(a, 3))
    for p, (axis, a, b) in enumerate(PARTS):
        sends.landed(over[p].at[5, high], 64 * p + 50)
        sends.landed(under[p].at[5, low], 64 * p + 51)
        sends.landed(over[p].at[5, low], 64 * p + 52)
        sends.landed(under[p].at[5, high], 64 * p + 53)
        columns = pl.ds(BEGIN[p], WIDTH[p])
        total = sums[p][0, 0].astype(F32) + over[p][5].astype(F32) + under[p][5].astype(F32)
        out_ref[:, columns] = (hidden_ref[:, columns].astype(F32) + total).astype(BF16)
    sends.finish()


def combine(rows, expert_gate, expert_up, expert_down, mix, hidden):
    vmem = pl.BlockSpec(memory_space=pltpu.VMEM)
    hbm = pl.BlockSpec(memory_space=pl.ANY)
    return pl.pallas_call(
        combine_kernel,
        out_shape=jax.ShapeDtypeStruct(hidden.shape, BF16),
        in_specs=[hbm] * 4 + [vmem] * 2,
        out_specs=vmem,
        scratch_shapes=[
            pltpu.VMEM(rows.shape, BF16),
            pltpu.VMEM((256, expert_gate.shape[2]), BF16),
            pltpu.VMEM(expert_gate.shape, BF16),
            pltpu.VMEM(expert_up.shape, BF16),
            pltpu.VMEM(expert_down.shape, BF16),
            pltpu.SemaphoreType.DMA((4,)),
            pltpu.SemaphoreType.DMA((3, 2)),
        ]
        + [pltpu.VMEM((8, 4, 4, 16, w), BF16) for w in WIDTH]
        + [pltpu.VMEM((4, 4, 16, w), BF16) for w in WIDTH] * 2
        + [pltpu.VMEM((4, 4, 128, w), BF16) for w in WIDTH]
        + [pltpu.VMEM((6, 128, w), BF16) for w in WIDTH] * 2
        + [pltpu.VMEM((2, 128, w), BF16) for w in WIDTH] * 2
        + [pltpu.SemaphoreType.DMA((208,)), pltpu.SemaphoreType.DMA((192,))],
        compiler_params=pltpu.CompilerParams(
            collective_id=2, has_side_effects=True, vmem_limit_bytes=58 * 1024 * 1024
        ),
        cost_estimate=pl.CostEstimate(flops=20_000_000_000, bytes_accessed=10_000_000, transcendentals=0),
    )(rows, expert_gate, expert_up, expert_down, mix, hidden)


def moe(hidden_state, normed, expert_ids, gate_weights, expert_gate, expert_up, expert_down):
    rows, mix = dispatch(normed, expert_ids.T, gate_weights.T)
    return combine(rows, expert_gate, expert_up, expert_down, mix, hidden_state)


def shards(
    residual_in,
    query_input,
    key_input,
    value_input,
    out_gate,
    write_strength,
    decay_rate,
    head_gain,
    out_proj,
    post_gain,
    expert_ids,
    gate_weights,
    expert_gate,
    expert_up,
    expert_down,
):
    stride = lax.axis_size("seq") // 4
    hidden_state, normed = mixer(
        query_input,
        key_input,
        value_input,
        out_gate,
        residual_in,
        out_proj,
        write_strength,
        decay_rate,
        head_gain,
        post_gain,
        stride,
    )
    return moe(hidden_state, normed, expert_ids, gate_weights, expert_gate, expert_up, expert_down)


def solution(mesh):
    both = ("seq", "exp")
    placed = (
        P(both, None),
        P(both, None),
        P(both, None),
        P(both, None),
        P(both, None),
        P(both, None),
        P(both, None),
        P(),
        P(None, "exp"),
        P(),
        P(both, None),
        P(both, None),
        P(both, None, None),
        P(both, None, None),
        P(both, None, None),
    )
    return jax.shard_map(shards, mesh=mesh, in_specs=placed, out_specs=P(both, None), check_vma=False)
```

profile of v0, /device:TPU:1, one launch (start us, length us, event | category | flops | bytes accessed | tf_op | source)
XLA Modules:
  0.0 253.4 jit_solution(2061492597283533670)
XLA Ops:
  0.0 76.4 %shard_map.145 = (bf16[128,2048]{1,0:T(8,128)(2,1)}, bf16[128,2048]{1,0:T(8,128)(2,1)}) custom-call(bf16[128,1024]{1,0:T(8,128)(2,1)} %q_hbm.1, bf16[128,1024]{1,0:T(8,128)(2,1)} %k_hbm.1, bf16[128,2048]{1,0:T(8,128)(2,1)} %v_hbm.1, bf16[128,2048]{1,0:T(8,128)(2,1)} %gate_hbm.2, bf16[128,2048]{1,0:T(8,128)(2,1)} %residual_hbm.1, bf16[2048,512]{1,0:T(8,128)(2,1)} %proj_hbm.1, ...), custom_call_target="tpu_custom_call" | custom-call | flops 8000000000 | bytes 4000000 | tf_op jit(solution)/shard_map/pallas_call | solution.py:506
  76.4 85.8 %shard_map.146 = (bf16[4,2,4,4,2,8,2048]{6,5,4,3,2,1,0:T(8,128)(2,1)}, bf16[3,16,128,128]{3,2,1,0:T(8,128)(2,1)}) custom-call(bf16[128,2048]{1,0:T(8,128)(2,1)} %get-tuple-element.9.normed_ref, s32[10,128]{1,0:T(8,128)} %bitcast.9, f32[10,128]{1,0:T(8,128)} %bitcast.10), custom_call_target="tpu_custom_call" | custom-call | flops 2000000000 | bytes 10000000 | tf_op jit(solution)/shard_map/pallas_call | solution.py:815
  162.2 89.3 %shard_map.147 = bf16[128,2048]{1,0:T(8,128)(2,1)} custom-call(bf16[4,2,4,4,2,8,2048]{6,5,4,3,2,1,0:T(8,128)(2,1)} %get-tuple-element.10.rows_hbm, bf16[2,2048,512]{2,1,0:T(8,128)(2,1)} %gate_hbm.3, bf16[2,2048,512]{2,1,0:T(8,128)(2,1)} %up_hbm.1, bf16[2,512,2048]{2,1,0:T(8,128)(2,1)} %down_hbm.1, bf16[3,16,128,128]{3,2,1,0:T(8,128)(2,1)} %get-tuple-element.11.mix_ref, ...), custom_call_target="tpu_custom_call" | custom-call | flops 20000000000 | bytes 10000000 | tf_op jit(solution)/shard_map/pallas_call | solution.py:1045
  251.5 1.9 copy.17
where the time goes:
time: 254 us; the launch traced here: 253 us
  Pallas kernels  251 us (99%)
    pallas_call x1, Pallas kernels, combine(): pl.pallas_call(combine_kernel, out_shape=jax.ShapeDtypeStruct(hidden.shap...  89.3 us
    pallas_call x1, Pallas kernels, dispatch(): pl.pallas_call(dispatch_kernel, out_shape=[jax.ShapeDtypeStruct((4, 2, 4,...  85.8 us
    pallas_call x1, Pallas kernels, mixer(): pl.pallas_call(partial(mixer_kernel, seq_size, exp_size, stride), out_sha...  76.4 us

commit v1 on v0

--- a/solution.py
+++ b/solution.py
@@ -89,6 +89,8 @@
     local_out,
     query_high,
     query_low,
+    newest_of,
+    key_of,
     maps,
     adds,
     maps_in,
@@ -266,15 +268,13 @@
 
     def key_head(kh):
         columns = pl.ds(pl.multiple_of(kh * DK, DK), DK)
-        k_raw, q_raw = k_ref[:, columns], q_ref[:, columns]
-        k_wide, q_wide = k_raw.astype(F32), q_raw.astype(F32)
+        k_raw = k_ref[:, columns]
+        k_wide = k_raw.astype(F32)
         k_inv = lax.rsqrt(jnp.sum(k_wide * k_wide, axis=1, keepdims=True) + 1e-6)
-        q_inv = lax.rsqrt(jnp.sum(q_wide * q_wide, axis=1, keepdims=True) + 1e-6) * DK ** (-0.5)
         k_inv = jnp.broadcast_to(k_inv, (128, 128))
         k_inv_row = k_inv.T
         k_t = k_wide.T.astype(BF16)
         gram = mm_t(k_raw, k_raw) * k_inv * k_inv_row
-        mixed = mm_t(q_raw, k_raw) * q_inv * k_inv_row
         for part in range(HV // HK):
             h = kh * (HV // HK) + part
             head_columns = pl.ds(pl.multiple_of(h * DV, DV), DV)
@@ -296,11 +296,27 @@
             maps[h] = jnp.where(row == col, jnp.exp(log_last), 0.0) - moved
             side = split(newest * fade)
             adds[h] = (mm(k_t, side[0]) + mm(k_t, side[1])).astype(BF16)
+            newest_of[h] = newest
+            key_of[h] = key_matrix
+
+    def local_head(kh, carry):
+        columns = pl.ds(pl.multiple_of(kh * DK, DK), DK)
+        k_raw, q_raw = k_ref[:, columns], q_ref[:, columns]
+        k_wide, q_wide = k_raw.astype(F32), q_raw.astype(F32)
+        k_inv = lax.rsqrt(jnp.sum(k_wide * k_wide, axis=1, keepdims=True) + 1e-6)
+        q_inv = lax.rsqrt(jnp.sum(q_wide * q_wide, axis=1, keepdims=True) + 1e-6) * DK ** (-0.5)
+        mixed = mm_t(q_raw, k_raw) * q_inv * jnp.broadcast_to(k_inv, (128, 128)).T
+        for part in range(HV // HK):
+            h = kh * (HV // HK) + part
+            log_row = rows_of(logs[pl.ds(h, 1), :])
+            log_col = log_row.T
+            ratio = jnp.where(row >= col, jnp.exp(jnp.where(row >= col, log_col - log_row, 0.0)), 0.0)
             mix = split(mixed * ratio)
-            local_out[h] = mm3(mix, split(newest))
-            effective = split(q_wide * q_inv * jnp.exp(log_col) - mm3(mix, split(key_matrix)))
+            local_out[h] = mm3(mix, split(newest_of[h]))
+            effective = split(q_wide * q_inv * jnp.exp(log_col) - mm3(mix, split(key_of[h])))
             query_high[h] = effective[0]
             query_low[h] = effective[1]
+        return carry
 
     def key_heads(step, carry):
         for part in range(TOGETHER):
@@ -385,6 +401,7 @@
         return carry
 
     lax.fori_loop(group + 1, groups, send_group, 0)
+    lax.fori_loop(0, HK, local_head, 0)
 
     for number in range(3):
         for copy in z_landing[number][2:]:
@@ -520,6 +537,8 @@
             pltpu.VMEM((HV,) + square, F32),
             pltpu.VMEM((HV,) + square, BF16),
             pltpu.VMEM((HV,) + square, BF16),
+            pltpu.VMEM((HV,) + square, F32),
+            pltpu.VMEM((HV,) + square, F32),
             pltpu.VMEM((HV,) + square, F32),
             pltpu.VMEM((HV,) + square, BF16),
             pltpu.VMEM((GROUP,) + square, F32),

time: 254 us -> 253 us (level)
  no operation moved by 1% of the time
where the time goes in v1:
time: 253 us; the launch traced here: 252 us
  Pallas kernels  250 us (99%)
    pallas_call x1, Pallas kernels, combine(): pl.pallas_call(combine_kernel, out_shape=jax.ShapeDtypeStruct(hidden.shap...  89.3 us
    pallas_call x1, Pallas kernels, dispatch(): pl.pallas_call(dispatch_kernel, out_shape=[jax.ShapeDtypeStruct((4, 2, 4,...  84 us
    pallas_call x1, Pallas kernels, mixer(): pl.pallas_call(partial(mixer_kernel, seq_size, exp_size, stride), out_sha...  77.1 us

profile of v1, /device:TPU:1, one launch (start us, length us, event | category | flops | bytes accessed | tf_op | source)
XLA Modules:
  0.0 252.3 jit_solution(7429636199829717338)
XLA Ops:
  0.0 77.1 %shard_map.145 = (bf16[128,2048]{1,0:T(8,128)(2,1)}, bf16[128,2048]{1,0:T(8,128)(2,1)}) custom-call(bf16[128,1024]{1,0:T(8,128)(2,1)} %q_hbm.1, bf16[128,1024]{1,0:T(8,128)(2,1)} %k_hbm.1, bf16[128,2048]{1,0:T(8,128)(2,1)} %v_hbm.1, bf16[128,2048]{1,0:T(8,128)(2,1)} %gate_hbm.2, bf16[128,2048]{1,0:T(8,128)(2,1)} %residual_hbm.1, bf16[2048,512]{1,0:T(8,128)(2,1)} %proj_hbm.1, ...), custom_call_target="tpu_custom_call" | custom-call | flops 8000000000 | bytes 4000000 | tf_op jit(solution)/shard_map/pallas_call | solution.py:523
  77.1 84.0 %shard_map.146 = (bf16[4,2,4,4,2,8,2048]{6,5,4,3,2,1,0:T(8,128)(2,1)}, bf16[3,16,128,128]{3,2,1,0:T(8,128)(2,1)}) custom-call(bf16[128,2048]{1,0:T(8,128)(2,1)} %get-tuple-element.9.normed_ref, s32[10,128]{1,0:T(8,128)} %bitcast.9, f32[10,128]{1,0:T(8,128)} %bitcast.10), custom_call_target="tpu_custom_call" | custom-call | flops 2000000000 | bytes 10000000 | tf_op jit(solution)/shard_map/pallas_call | solution.py:834
  161.1 89.3 %shard_map.147 = bf16[128,2048]{1,0:T(8,128)(2,1)} custom-call(bf16[4,2,4,4,2,8,2048]{6,5,4,3,2,1,0:T(8,128)(2,1)} %get-tuple-element.10.rows_hbm, bf16[2,2048,512]{2,1,0:T(8,128)(2,1)} %gate_hbm.3, bf16[2,2048,512]{2,1,0:T(8,128)(2,1)} %up_hbm.1, bf16[2,512,2048]{2,1,0:T(8,128)(2,1)} %down_hbm.1, bf16[3,16,128,128]{3,2,1,0:T(8,128)(2,1)} %get-tuple-element.11.mix_ref, ...), custom_call_target="tpu_custom_call" | custom-call | flops 20000000000 | bytes 10000000 | tf_op jit(solution)/shard_map/pallas_call | solution.py:1064
  250.4 1.9 copy.17
